TPU v7x, 32 devices: a whole 2x2x4 slice. The times are simulated.
32 devices in a mesh: dp: 2 (over y), fsdp: 4 (over x, core), tensor: 4 (over z).
Axes of the slice: x: 2, y: 2, z: 4, core: 2. Of those that a mesh axis runs over, the one named last changes fastest.
Arguments:
- activations: bfloat16 [1024, 8192], P(('dp', 'fsdp'), 'tensor'), may hold values from -6 to 6
- cotangent: bfloat16 [1024, 8192], P(('dp', 'fsdp'), 'tensor'), may hold values from -6 to 6
- up_tiles: bfloat16 [1024, 128, 128], P(('fsdp', 'tensor')), may hold values from -0.1875 to 0.1875
- down_tiles: bfloat16 [1024, 128, 128], P(('fsdp', 'tensor')), may hold values from -0.125 to 0.125
- up_rows: int32 [256, 4], P(None, 'tensor'), may hold values from 0 to 63, as said below
- up_cols: int32 [256, 4], P(None, 'tensor'), may hold values from 0 to 31, as said below
- down_rows: int32 [256, 4], P(None, 'tensor'), may hold values from 0 to 31, as said below
- down_cols: int32 [256, 4], P(None, 'tensor'), may hold values from 0 to 63, as said below
Outputs:
- output: bfloat16 [1024, 8192], P(('dp', 'fsdp'), 'tensor')
- input_grad: bfloat16 [1024, 8192], P(('dp', 'fsdp'), 'tensor')
- up_grad: float32 [1024, 128, 128], P(('fsdp', 'tensor'))
- down_grad: float32 [1024, 128, 128], P(('fsdp', 'tensor'))
Inputs may be any that keep to these rules, and one draw needn't show every extreme that they name: `up_rows`: within a column, the up tiles of one hidden-unit block name distinct feature blocks. `up_cols`: every value occurs exactly 8 times in each column. `down_rows`: every value occurs exactly 8 times in each column. `down_cols`: within a column, the down tiles of one hidden-unit block name distinct feature blocks.
All inputs are finite; a program needn't handle non-finite values.
Results may differ from a plain program's by a relative error of at most 0.018.
Values may be sent and summed in bfloat16 or wider, within the bound.
A program may use at most 128 MiB of HBM per device.

v0:
```python
import jax
import jax.numpy as jnp
from jax import lax
from jax.sharding import PartitionSpec as P

D = 8192
FF = 16384
inv_root_two = 0.7071067811865476
inv_root_tau = 0.3989422804014327


def gelu_parts(values):
    normal_cdf = 0.5 * (1.0 + jax.scipy.special.erf(values * inv_root_two))
    density = inv_root_tau * jnp.exp(-0.5 * values * values)
    return (values * normal_cdf, normal_cdf + values * density)


def grouped_pick(acting, far_index, hidden_blocks, block_size):
    rows_here = acting.shape[0]
    picked = acting.reshape(rows_here, -1, block_size)[:, far_index]
    return picked.reshape(rows_here, hidden_blocks, -1, block_size)


def add_far(product, far_index, model_blocks):
    rows_here = product.shape[0]
    block_size = product.shape[-1]
    flat = product.reshape(rows_here, -1, block_size)
    summed = (
        jnp.zeros((rows_here, model_blocks, block_size), jnp.float32).at[:, far_index].add(flat)
    )
    return summed.reshape(rows_here, model_blocks * block_size)


def grouped_tiles(tiles, order, hidden_blocks):
    block_size = tiles.shape[1]
    return tiles[order].reshape(hidden_blocks, -1, block_size, block_size)


def body(activations, cotangent, up_tiles, down_tiles, up_rows, up_cols, down_rows, down_cols):
    block_size = up_tiles.shape[1]
    hidden_blocks = FF // (block_size * lax.axis_size("tensor"))
    model_blocks = D // block_size
    up_order = jnp.argsort(up_cols[:, 0], stable=True)
    down_order = jnp.argsort(down_rows[:, 0], stable=True)
    up_back = jnp.argsort(up_order)
    down_back = jnp.argsort(down_order)
    up_far = up_rows[:, 0][up_order]
    down_far = down_cols[:, 0][down_order]
    full_input = lax.all_gather(activations, "tensor", axis=1, tiled=True)
    input_pick = grouped_pick(full_input, up_far, hidden_blocks, block_size)
    up_whole = lax.all_gather(up_tiles, "fsdp", axis=0, tiled=True)
    up_sorted = grouped_tiles(up_whole, up_order, hidden_blocks)
    pre_act = jnp.einsum(
        "thkb,hkbc->thc", input_pick, up_sorted, preferred_element_type=jnp.float32
    )
    gelu_out, gelu_slope = gelu_parts(pre_act)
    hidden = gelu_out.astype(jnp.bfloat16)
    down_whole = lax.all_gather(down_tiles, "fsdp", axis=0, tiled=True)
    down_sorted = grouped_tiles(down_whole, down_order, hidden_blocks)
    out_product = jnp.einsum(
        "thb,hkbc->thkc", hidden, down_sorted, preferred_element_type=jnp.float32
    )
    partial_out = add_far(out_product, down_far, model_blocks)
    output = lax.psum_scatter(
        partial_out.astype(jnp.bfloat16), "tensor", scatter_dimension=1, tiled=True
    )
    full_cotangent = lax.all_gather(cotangent, "tensor", axis=1, tiled=True)
    cot_pick = grouped_pick(full_cotangent, down_far, hidden_blocks, block_size)
    hidden_grad = jnp.einsum(
        "thkc,hkbc->thb", cot_pick, down_sorted, preferred_element_type=jnp.float32
    )
    pre_grad = (hidden_grad * gelu_slope).astype(jnp.bfloat16)
    in_product = jnp.einsum(
        "thc,hkbc->thkb", pre_grad, up_sorted, preferred_element_type=jnp.float32
    )
    partial_in = add_far(in_product, up_far, model_blocks)
    input_grad = lax.psum_scatter(
        partial_in.astype(jnp.bfloat16), "tensor", scatter_dimension=1, tiled=True
    )
    up_grouped = jnp.einsum(
        "thkb,thc->hkbc", input_pick, pre_grad, preferred_element_type=jnp.float32
    )
    down_grouped = jnp.einsum(
        "thb,thkc->hkbc", hidden, cot_pick, preferred_element_type=jnp.float32
    )
    up_rounded = up_grouped.astype(jnp.bfloat16).reshape(-1, block_size, block_size)
    down_rounded = down_grouped.astype(jnp.bfloat16).reshape(-1, block_size, block_size)
    up_term = up_rounded[up_back].astype(jnp.float32)
    down_term = down_rounded[down_back].astype(jnp.float32)
    replicas = lax.axis_size("dp")
    owners = lax.axis_size("fsdp")

    def regroup(grad_term):
        per_piece = grad_term.shape[0] // (replicas * owners)
        shaped = grad_term.reshape(owners, replicas, per_piece, block_size, block_size)
        return shaped.transpose(1, 0, 2, 3, 4).reshape(-1, block_size, block_size)

    up_piece, down_piece = (
        lax.psum_scatter(
            regroup(up_term).astype(jnp.bfloat16), ("dp", "fsdp"), scatter_dimension=0, tiled=True
        ).astype(jnp.float32),
        lax.psum_scatter(
            regroup(down_term).astype(jnp.bfloat16), ("dp", "fsdp"), scatter_dimension=0, tiled=True
        ).astype(jnp.float32),
    )
    up_grad, down_grad = (
        lax.all_gather(up_piece.astype(jnp.bfloat16), "dp", axis=0, tiled=True).astype(
            up_piece.dtype
        ),
        lax.all_gather(down_piece.astype(jnp.bfloat16), "dp", axis=0, tiled=True).astype(
            down_piece.dtype
        ),
    )
    return (output, input_grad, up_grad, down_grad)


def solution(mesh):
    in_specs = (
        P(("dp", "fsdp"), "tensor"),
        P(("dp", "fsdp"), "tensor"),
        P(("fsdp", "tensor"), None, None),
        P(("fsdp", "tensor"), None, None),
        P(None, "tensor"),
        P(None, "tensor"),
        P(None, "tensor"),
        P(None, "tensor"),
    )
    out_specs = (
        P(("dp", "fsdp"), "tensor"),
        P(("dp", "fsdp"), "tensor"),
        P(("fsdp", "tensor"), None, None),
        P(("fsdp", "tensor"), None, None),
    )
    return jax.shard_map(body, mesh=mesh, in_specs=in_specs, out_specs=out_specs, check_vma=False)
```

profile of v0, /device:TPU:0, one launch (start us, length us, event | category | flops | bytes accessed | tf_op | source)
XLA Modules:
  0.0 582.8 jit_solution(14450266587126344888)
XLA Ops:
  12.8 3.8 sort.62
  16.6 3.2 sort.65
  19.8 3.8 sort.63
  27.7 32.2 %all-gather.11.cloned.1.call-done = bf16[128,8192]{0,1:T(8,128)(2,1)} async-done(((bf16[128,2048]{0,1:T(8,128)(2,1)}), bf16[128,8192]{0,1:T(8,128)(2,1)}) %all-gather.11.cloned.1.call-update) | async-done | bytes 2097168 | tf_op jit(solution)/shard_map/all_gather | solution.py:49
  59.9 3.2 copy.63
  63.1 43.5 %all-gather.13.cloned.1.call-done = bf16[128,8192]{0,1:T(8,128)(2,1)} async-done(((bf16[128,2048]{0,1:T(8,128)(2,1)}), bf16[128,8192]{0,1:T(8,128)(2,1)}) %all-gather.13.cloned.1.call-update) | async-done | bytes 2097168 | tf_op jit(solution)/shard_map/all_gather | solution.py:67
  106.6 4.1 copy.70
  110.7 10.3 %gather_fusion.5 = bf16[256,128,128]{2,1,0:T(8,128)(2,1)} fusion(bf16[128,64,128]{2,0,1:T(8,128)(2,1)} %copy.70, s32[1024]{0:T(1024)S(1)} %pad_clamp_fusion.2), kind=kCustom, calls=%fused_computation.5 | custom fusion | bytes 16778240 | tf_op jit(solution)/shard_map/gather | solution.py:20
  121.0 8.6 %gather_fusion.4 = bf16[256,128,128]{2,1,0:T(8,128)(2,1)} fusion(bf16[128,64,128]{2,0,1:T(8,128)(2,1)S(1)} %copy.63, s32[1024]{0:T(1024)S(1)} %pad_clamp_fusion.3), kind=kCustom, calls=%fused_computation.4 | custom fusion | bytes 16778240 | tf_op jit(solution)/shard_map/gather | solution.py:20
  129.6 35.7 %all-gather.9.cloned.1.call-done = bf16[256,128,128]{2,1,0:T(8,128)(2,1)} async-done(((bf16[64,128,128]{2,1,0:T(8,128)(2,1)}), bf16[256,128,128]{2,1,0:T(8,128)(2,1)}) %all-gather.9.cloned.1.call-update) | async-done | bytes 8388624 | tf_op jit(solution)/shard_map/all_gather | solution.py:51
  165.3 13.5 %gather_fusion.2 = bf16[256,128,128]{2,1,0:T(8,128)(2,1)} fusion(bf16[256,128,128]{2,1,0:T(8,128)(2,1)} %all-gather.9.cloned.1.call-done, s32[1024]{0:T(1024)S(1)} %pad_clamp_fusion.4), kind=kCustom, calls=%fused_computation.2 | custom fusion | bytes 16778240 | tf_op jit(solution)/shard_map/gather | solution.py:36
  178.8 8.3 %fusion.15 = f32[32,128,128,1]{2,1,3,0:T(8,128)S(1)} fusion(bf16[32,8,128,128]{3,2,1,0:T(8,128)(2,1)} %bitcast.97, bf16[128,32,8,128]{3,0,2,1:T(8,128)(2,1)} %bitcast.99), kind=kOutput, calls=%fused_computation.40 | convolution fusion | flops 1073741824 | bytes 18874368 | tf_op jit(solution)/shard_map/thkb,hkbc->thc/dot_general | solution.py:53
  187.1 9.3 %convolution_convert_fusion = bf16[32,8,128,128]{3,2,1,0:T(8,128)(2,1)} fusion(bf16[128,32,8,128]{3,0,2,1:T(8,128)(2,1)} %bitcast.106, f32[32,128,128,1]{2,1,3,0:T(8,128)S(1)} %fusion.15), kind=kOutput, calls=%fused_computation.10 | convolution fusion | flops 1080557568 | bytes 18874368 | tf_op jit(solution)/shard_map/thb,thkc->hkbc/dot_general | solution.py:83
  196.5 12.1 %gather_fusion.7 = bf16[256,128,128]{1,2,0:T(8,128)(2,1)} fusion(bf16[256,128,128]{1,2,0:T(8,128)(2,1)} %bitcast.113, s32[1024]{0:T(1024)S(1)} %pad_clamp_fusion), kind=kCustom, calls=%fused_computation.7 | custom fusion | bytes 16778240 | tf_op jit(solution)/shard_map/gather | solution.py:89
  208.5 12.0 %copy.79 = bf16[4,2,32,128,128]{4,3,2,0,1:T(8,128)(2,1)} copy(bf16[4,2,32,128,128]{3,4,2,1,0:T(8,128)(2,1)} %bitcast.110) | data formatting | bytes 16777216 | tf_op jit(solution)/shard_map/convert_element_type | solution.py:103
  220.6 3.2 sort.64
  225.0 12.7 %gather_fusion.1 = bf16[256,128,128]{2,1,0:T(8,128)(2,1)} fusion(bf16[256,128,128]{2,1,0:T(8,128)(2,1)} %all-gather.7.cloned.1.call-done, s32[1024]{0:T(1024)S(1)} %pad_clamp_fusion.5), kind=kCustom, calls=%fused_computation.1 | custom fusion | bytes 16778240 | tf_op jit(solution)/shard_map/gather | solution.py:36
  237.7 10.7 %fusion.10 = bf16[128,32,128,1]{0,2,3,1:T(8,128)(2,1)S(1)} fusion(f32[32,128,128,1]{2,1,3,0:T(8,128)S(1)} %fusion.15, bf16[32,8,128,128]{3,2,1,0:T(8,128)(2,1)} %bitcast.108, bf16[128,32,8,128]{3,0,2,1:T(8,128)(2,1)} %bitcast.107), kind=kOutput, calls=%fused_computation.25 | convolution fusion | flops 1078984704 | bytes 19922944 | tf_op jit(solution)/shard_map/thkc,hkbc->thb/dot_general | solution.py:69
  248.4 9.1 %convolution_convert_fusion.1 = bf16[32,8,128,128]{3,2,1,0:T(8,128)(2,1)} fusion(bf16[128,32,8,128]{3,0,2,1:T(8,128)(2,1)} %bitcast.100, bf16[128,32,128,1]{0,2,3,1:T(8,128)(2,1)S(1)} %fusion.10), kind=kOutput, calls=%fused_computation.11 | convolution fusion | flops 1077936128 | bytes 17825792 | tf_op jit(solution)/shard_map/thkb,thc->hkbc/dot_general | solution.py:80
  257.5 12.2 %gather_fusion.6 = bf16[256,128,128]{2,1,0:T(8,128)(2,1)} fusion(bf16[256,128,128]{2,1,0:T(8,128)(2,1)} %bitcast.111, s32[1024]{0:T(1024)S(1)} %pad_clamp_fusion.1), kind=kCustom, calls=%fused_computation.6 | custom fusion | bytes 16778240 | tf_op jit(solution)/shard_map/gather | solution.py:88
  269.7 10.4 %copy.76 = bf16[4,2,32,128,128]{4,3,2,0,1:T(8,128)(2,1)} copy(bf16[4,2,32,128,128]{4,3,2,1,0:T(8,128)(2,1)} %bitcast.112) | data formatting | bytes 16777216 | tf_op jit(solution)/shard_map/convert_element_type | solution.py:100
  280.4 11.6 %fusion.13 = f32[32,8,128,128]{3,2,1,0:T(8,128)} fusion(bf16[32,8,128,128]{3,2,1,0:T(8,128)(2,1)} %bitcast.109, f32[32,128,128,1]{2,1,3,0:T(8,128)S(1)} %fusion.15), kind=kOutput, calls=%fused_computation.39 | convolution fusion | flops 1076363264 | bytes 27262976 | tf_op jit(solution)/shard_map/thb,hkbc->thkc/dot_general | solution.py:60
  292.0 17.5 %copy.67 = f32[128,256,128]{2,0,1:T(8,128)} copy(f32[128,256,128]{0,2,1:T(8,128)} %bitcast.103) | data formatting | bytes 33554432 | tf_op jit(solution)/shard_map/reshape | solution.py:27
  312.2 52.3 %scatter_fusion = f32[128,64,128]{2,0,1:T(8,128)} fusion(f32[128,64,128]{2,0,1:T(8,128)} %broadcast.42.clone, s32[256]{0:T(256)S(1)} %bitcast.121, f32[256,128,128]{2,1,0:T(8,128)} %bitcast.102), kind=kCustom, calls=%fused_computation.8 | custom fusion | flops 4194304 | bytes 50332672 | tf_op jit(solution)/shard_map/scatter-add | solution.py:29
  370.1 11.5 %fusion.16 = f32[32,8,128,128]{3,2,1,0:T(8,128)} fusion(bf16[32,8,128,128]{3,2,1,0:T(8,128)(2,1)} %bitcast.98, bf16[128,32,128,1]{0,2,3,1:T(8,128)(2,1)S(1)} %fusion.10), kind=kOutput, calls=%fused_computation.41 | convolution fusion | flops 1073741824 | bytes 26214400 | tf_op jit(solution)/shard_map/thc,hkbc->thkb/dot_general | solution.py:73
  381.6 17.5 %copy.72 = f32[128,256,128]{2,0,1:T(8,128)} copy(f32[128,256,128]{0,2,1:T(8,128)} %bitcast.96) | data formatting | bytes 33554432 | tf_op jit(solution)/shard_map/reshape | solution.py:27
  401.7 51.3 %scatter_fusion.1 = f32[128,64,128]{2,0,1:T(8,128)} fusion(f32[128,64,128]{2,0,1:T(8,128)} %broadcast.42.clone.1, s32[256]{0:T(256)S(1)} %bitcast.119, f32[256,128,128]{2,1,0:T(8,128)} %bitcast.101), kind=kCustom, calls=%fused_computation.9 | custom fusion | flops 4194304 | bytes 50332672 | tf_op jit(solution)/shard_map/scatter-add | solution.py:29
  461.9 41.3 %reduce-scatter.7.cloned.1.call-done = bf16[128,2048]{0,1:T(8,128)(2,1)} async-done(((bf16[128,8192]{0,1:T(8,128)(2,1)}), bf16[128,2048]{0,1:T(8,128)(2,1)}) %reduce-scatter.7.cloned.1.call-update) | async-done | bytes 524304 | tf_op jit(solution)/shard_map/reduce_scatter | solution.py:77
  505.2 31.8 %all-gather.17.cloned.1.call-done = bf16[64,128,128]{2,1,0:T(8,128)(2,1)} async-done(((bf16[32,128,128]{2,1,0:T(8,128)(2,1)}), bf16[64,128,128]{2,1,0:T(8,128)(2,1)}) %all-gather.17.cloned.1.call-update) | async-done | bytes 2097168 | tf_op jit(solution)/shard_map/all_gather | solution.py:110
  537.1 4.1 convert_element_type.79
  541.2 30.4 %all-gather.15.cloned.1.call-done = bf16[64,128,128]{2,1,0:T(8,128)(2,1)} async-done(((bf16[32,128,128]{2,1,0:T(8,128)(2,1)}), bf16[64,128,128]{2,1,0:T(8,128)(2,1)}) %all-gather.15.cloned.1.call-update) | async-done | bytes 2097168 | tf_op jit(solution)/shard_map/all_gather | solution.py:107
  571.6 4.1 convert_element_type.73
  (58 shorter events, 32.7 us)
Async XLA Ops:
  7.2 16.5 %copy-start = (s32[256,1]{0,1:T(1,128)S(1)}, s32[256,1]{0,1:T(1,128)}, u32[]{:S(2)}) copy-start(s32[256,1]{0,1:T(1,128)} %param.12) | copy-start | bytes 3076
  7.2 18.5 %copy-start.2 = (s32[256,1]{0,1:T(1,128)S(1)}, s32[256,1]{0,1:T(1,128)}, u32[]{:S(2)}) copy-start(s32[256,1]{0,1:T(1,128)} %param.15) | copy-start | bytes 3076
  7.2 52.7 %all-gather.11.cloned.1.call-start = ((), (), s32[]{:S(2)}) async-start(), calls=%async_computation.6 | async-start | bytes 2621440 | tf_op jit(solution)/shard_map/all_gather | solution.py:49
  9.3 97.3 %all-gather.13.cloned.1.call-start = ((), (), s32[]{:S(2)}) async-start(), calls=%async_computation.8 | async-start | bytes 2621440 | tf_op jit(solution)/shard_map/all_gather | solution.py:67
  11.4 153.9 %all-gather.9.cloned.1.call-start = ((), (), s32[]{:S(2)}) async-start(), calls=%async_computation.5 | async-start | bytes 10485760 | tf_op jit(solution)/shard_map/all_gather | solution.py:51
  12.2 212.8 %all-gather.7.cloned.1.call-start = ((), (), s32[]{:S(2)}) async-start(), calls=%async_computation.4 | async-start | bytes 10485760 | tf_op jit(solution)/shard_map/all_gather | solution.py:58
  12.7 445.8 %reduce-scatter.11.cloned.1.call-start = ((), (), s32[]{:S(2)}) async-start(), calls=%async_computation.12 | async-start | bytes 9437184 | tf_op jit(solution)/shard_map/reduce_scatter | solution.py:102
  220.5 238.7 %reduce-scatter.9.cloned.1.call-start = ((), (), s32[]{:S(2)}) async-start(), calls=%async_computation.10 | async-start | bytes 9437184 | tf_op jit(solution)/shard_map/reduce_scatter | solution.py:99
  280.1 179.7 %reduce-scatter.5.cloned.1.call-start = ((), (), s32[]{:S(2)}) async-start(), calls=%async_computation.7 | async-start | bytes 2621440 | tf_op jit(solution)/shard_map/reduce_scatter | solution.py:64
  370.1 133.1 %reduce-scatter.7.cloned.1.call-start = ((), (), s32[]{:S(2)}) async-start(), calls=%async_computation.9 | async-start | bytes 2621440 | tf_op jit(solution)/shard_map/reduce_scatter | solution.py:77
  458.5 78.6 %all-gather.17.cloned.1.call-start = ((), (), s32[]{:S(2)}) async-start(), calls=%async_computation.13 | async-start | bytes 3145728 | tf_op jit(solution)/shard_map/all_gather | solution.py:110
  458.5 117.2 %copy-start.1 = (s32[256,1]{0,1:T(1,128)S(1)}, s32[256,1]{0,1:T(1,128)}, u32[]{:S(2)}) copy-start(s32[256,1]{0,1:T(1,128)} %param.12) | copy-start | bytes 3076
  459.2 112.4 %all-gather.15.cloned.1.call-start = ((), (), s32[]{:S(2)}) async-start(), calls=%async_computation.11 | async-start | bytes 3145728 | tf_op jit(solution)/shard_map/all_gather | solution.py:107
Sparse Core Ops, SparseCore 0:
  10.1 49.7 all-gather.10
  62.1 44.5 all-gather.12
  108.2 57.0 all-gather.8
  166.7 58.2 all-gather.6
  228.3 71.5 reduce-scatter.10
  303.3 71.5 reduce-scatter.8
  377.7 43.6 reduce-scatter.4
  458.6 44.5 reduce-scatter.6
  504.7 32.2 all-gather.16
  538.5 33.0 all-gather.14
where the time goes:
time: 593 us; the launch traced here: 583 us
  waiting for transfers between devices  219 us (37%)
  local copies, waits for them, and re-layouts  157 us (26%)
  other arithmetic  131 us (22%)
  matrix products  60.6 us (10%)
  between operations  14.6 us (2%)
    scatter-add x2, other arithmetic, add_far(): jnp.zeros((rows_here, model_blocks, block_size), jnp.float32)  104 us
    all_gather x1, waiting for transfers between devices, body(): full_cotangent = lax.all_gather(cotangent, 'tensor', axis=1, tiled=True)  43.5 us
    reduce_scatter x1, waiting for transfers between devices, body(): lax.psum_scatter(partial_in.astype(jnp.bfloat16), 'tensor', scatter_dimen...  41.3 us
    all_gather x1, waiting for transfers between devices, body(): up_whole = lax.all_gather(up_tiles, 'fsdp', axis=0, tiled=True)  35.7 us
    reshape x2, local copies, waits for them, and re-layouts, add_far(): flat = product.reshape(rows_here, -1, block_size)  35 us
    all_gather x1, waiting for transfers between devices, body(): full_input = lax.all_gather(activations, 'tensor', axis=1, tiled=True)  32.2 us
    all_gather x1, waiting for transfers between devices, body(): lax.all_gather(down_piece.astype(jnp.bfloat16), 'dp', axis=0, tiled=True)  31.8 us
    all_gather x1, waiting for transfers between devices, body(): lax.all_gather(up_piece.astype(jnp.bfloat16), 'dp', axis=0, tiled=True)  30.4 us
  transfers between devices with their start and end apart: 10, of which 7 were waited for; matrix products, arithmetic and copies ran while one was open for 59% of the time, Pallas kernels for 0%

commit v1 on v0

--- a/solution.py
+++ b/solution.py
@@ -7,6 +7,16 @@
 FF = 16384
 inv_root_two = 0.7071067811865476
 inv_root_tau = 0.3989422804014327
+
+
+def pass_along(array, mesh_axis, dim):
+    size = lax.axis_size(mesh_axis)
+    held, blocks = (array, [array])
+    for _ in range(size - 1):
+        held = lax.ppermute(held, mesh_axis, [(i, (i + 1) % size) for i in range(size)])
+        blocks.insert(0, held)
+    row_of_blocks = jnp.concatenate(blocks, axis=dim)
+    return jnp.roll(row_of_blocks, (lax.axis_index(mesh_axis) + 1) * array.shape[dim], axis=dim)
 
 
 def gelu_parts(values):
@@ -64,7 +74,7 @@
     output = lax.psum_scatter(
         partial_out.astype(jnp.bfloat16), "tensor", scatter_dimension=1, tiled=True
     )
-    full_cotangent = lax.all_gather(cotangent, "tensor", axis=1, tiled=True)
+    full_cotangent = pass_along(cotangent, "tensor", 1)
     cot_pick = grouped_pick(full_cotangent, down_far, hidden_blocks, block_size)
     hidden_grad = jnp.einsum(
         "thkc,hkbc->thb", cot_pick, down_sorted, preferred_element_type=jnp.float32

time: 593 us -> 563 us (0.949)
  waiting for transfers between devices: 219 us -> 172 us
  starting transfers between devices: 0.61 us -> 20.4 us
    all_gather x1 -> x0, waiting for transfers between devices: 43.5 us -> none  [body(): full_cotangent = lax.all_gather(cotangent, 'tensor', axis=1, tiled=True)]
    ppermute x0 -> x3, waiting for transfers between devices: none -> 36.8 us  [pass_along(): lax.ppermute(held, mesh_axis, [(i, (i + 1) % size) for i in range(size)])]
    all_gather x1, waiting for transfers between devices: 32.2 us -> 0.01 us  [body(): full_input = lax.all_gather(activations, 'tensor', axis=1, tiled=True)]
    ppermute x0 -> x3, starting transfers between devices: none -> 19.8 us  [pass_along(): lax.ppermute(held, mesh_axis, [(i, (i + 1) % size) for i in range(size)])]
    all_gather x1, waiting for transfers between devices: 35.7 us -> 24.3 us  [body(): up_whole = lax.all_gather(up_tiles, 'fsdp', axis=0, tiled=True)]
  transfers between devices with their start and end apart: 10 -> 12, of which waited for: 7 -> 8; matrix products, arithmetic and copies ran while one was open for 59% -> 62% of each run, Pallas kernels for 0% -> 0%
where the time goes in v1:
time: 563 us; the launch traced here: 552 us
  waiting for transfers between devices  172 us (31%)
  local copies, waits for them, and re-layouts  155 us (28%)
  other arithmetic  130 us (23%)
  matrix products  60.6 us (11%)
  starting transfers between devices  20.4 us (4%)
  between operations  14.3 us (3%)
    scatter-add x2, other arithmetic, add_far(): jnp.zeros((rows_here, model_blocks, block_size), jnp.float32)  104 us
    reduce_scatter x1, waiting for transfers between devices, body(): lax.psum_scatter(partial_in.astype(jnp.bfloat16), 'tensor', scatter_dimen...  40.6 us
    ppermute x3, waiting for transfers between devices, pass_along(): lax.ppermute(held, mesh_axis, [(i, (i + 1) % size) for i in range(size)])  36.8 us
    reshape x2, local copies, waits for them, and re-layouts, add_far(): flat = product.reshape(rows_here, -1, block_size)  35.1 us
    all_gather x1, waiting for transfers between devices, body(): lax.all_gather(down_piece.astype(jnp.bfloat16), 'dp', axis=0, tiled=True)  31.9 us
    all_gather x1, waiting for transfers between devices, body(): lax.all_gather(up_piece.astype(jnp.bfloat16), 'dp', axis=0, tiled=True)  30.5 us
    gather x2, local copies, waits for them, and re-layouts, grouped_tiles(): return tiles[order].reshape(hidden_blocks, -1, block_size, block_size)  26.1 us
    all_gather x1, waiting for transfers between devices, body(): up_whole = lax.all_gather(up_tiles, 'fsdp', axis=0, tiled=True)  24.3 us
  transfers between devices with their start and end apart: 12, of which 8 were waited for; matrix products, arithmetic and copies ran while one was open for 62% of the time, Pallas kernels for 0%

profile of v1, /device:TPU:0, one launch (start us, length us, event | category | flops | bytes accessed | tf_op | source)
XLA Modules:
  0.0 552.3 jit_solution(6361769145240228448)
XLA Ops:
  17.5 3.2 sort.65
  29.7 5.7 %collective-permute-start.1 = (bf16[128,2048]{0,1:T(8,128)(2,1)S(1)}, bf16[128,2048]{0,1:T(8,128)(2,1)S(1)}, u32[]{:S(2)}, u32[]{:S(2)}) collective-permute-start(bf16[128,2048]{0,1:T(8,128)(2,1)S(1)} %collective-permute-done), channel_id=1, source_target_pairs={{0,1},{1,2},{2,3},{3,0},{4,5},{5,6},{6,7},{7,4},{8,9},{9,10},{10,1... | collective-permute-start | bytes 1572872 | tf_op jit(solution)/shard_map/ppermute | solution.py:16
  37.4 22.8 %collective-permute-done.1 = bf16[128,2048]{0,1:T(8,128)(2,1)S(1)} collective-permute-done((bf16[128,2048]{0,1:T(8,128)(2,1)S(1)}, bf16[128,2048]{0,1:T(8,128)(2,1)S(1)}, u32[]{:S(2)}, u32[]{:S(2)}) %collective-permute-start.1) | collective-permute-done | bytes 524320 | tf_op jit(solution)/shard_map/ppermute | solution.py:16
  60.2 10.9 %collective-permute-start.2 = (bf16[128,2048]{0,1:T(8,128)(2,1)S(1)}, bf16[128,2048]{0,1:T(8,128)(2,1)S(1)}, u32[]{:S(2)}, u32[]{:S(2)}) collective-permute-start(bf16[128,2048]{0,1:T(8,128)(2,1)S(1)} %collective-permute-done.1), channel_id=1, source_target_pairs={{0,1},{1,2},{2,3},{3,0},{4,5},{5,6},{6,7},{7,4},{8,9},{9,10},{10,1... | collective-permute-start | bytes 1572872 | tf_op jit(solution)/shard_map/ppermute | solution.py:16
  71.2 13.3 %collective-permute-done.2 = bf16[128,2048]{0,1:T(8,128)(2,1)S(1)} collective-permute-done((bf16[128,2048]{0,1:T(8,128)(2,1)S(1)}, bf16[128,2048]{0,1:T(8,128)(2,1)S(1)}, u32[]{:S(2)}, u32[]{:S(2)}) %collective-permute-start.2) | collective-permute-done | bytes 524320 | tf_op jit(solution)/shard_map/ppermute | solution.py:16
  86.6 3.5 copy.73
  90.1 8.6 %gather_fusion.5 = bf16[256,128,128]{2,1,0:T(8,128)(2,1)} fusion(bf16[128,64,128]{2,0,1:T(8,128)(2,1)S(1)} %copy.73, s32[1024]{0:T(1024)S(1)} %pad_clamp_fusion.2), kind=kCustom, calls=%fused_computation.5 | custom fusion | bytes 16778240 | tf_op jit(solution)/shard_map/gather | solution.py:30
  98.7 3.2 copy.64
  101.9 8.6 %gather_fusion.4 = bf16[256,128,128]{2,1,0:T(8,128)(2,1)} fusion(bf16[128,64,128]{2,0,1:T(8,128)(2,1)S(1)} %copy.64, s32[1024]{0:T(1024)S(1)} %pad_clamp_fusion.3), kind=kCustom, calls=%fused_computation.4 | custom fusion | bytes 16778240 | tf_op jit(solution)/shard_map/gather | solution.py:30
  110.6 24.3 %all-gather.8.cloned.1.call-done = bf16[256,128,128]{2,1,0:T(8,128)(2,1)} async-done(((bf16[64,128,128]{2,1,0:T(8,128)(2,1)}), bf16[256,128,128]{2,1,0:T(8,128)(2,1)}) %all-gather.8.cloned.1.call-update) | async-done | bytes 8388624 | tf_op jit(solution)/shard_map/all_gather | solution.py:61
  134.9 13.4 %gather_fusion.2 = bf16[256,128,128]{2,1,0:T(8,128)(2,1)} fusion(bf16[256,128,128]{2,1,0:T(8,128)(2,1)} %all-gather.8.cloned.1.call-done, s32[1024]{0:T(1024)S(1)} %pad_clamp_fusion.4), kind=kCustom, calls=%fused_computation.2 | custom fusion | bytes 16778240 | tf_op jit(solution)/shard_map/gather | solution.py:46
  148.3 8.4 %fusion.15 = f32[32,128,128,1]{2,1,3,0:T(8,128)S(1)} fusion(bf16[32,8,128,128]{3,2,1,0:T(8,128)(2,1)} %bitcast.97, bf16[128,32,8,128]{3,0,2,1:T(8,128)(2,1)} %bitcast.99), kind=kOutput, calls=%fused_computation.49 | convolution fusion | flops 1073741824 | bytes 18874368 | tf_op jit(solution)/shard_map/thkb,hkbc->thc/dot_general | solution.py:63
  156.7 9.3 %convolution_convert_fusion = bf16[32,8,128,128]{3,2,1,0:T(8,128)(2,1)} fusion(bf16[128,32,8,128]{3,0,2,1:T(8,128)(2,1)} %bitcast.106, f32[32,128,128,1]{2,1,3,0:T(8,128)S(1)} %fusion.15), kind=kOutput, calls=%fused_computation.10 | convolution fusion | flops 1080557568 | bytes 18874368 | tf_op jit(solution)/shard_map/thb,thkc->hkbc/dot_general | solution.py:93
  166.1 12.1 %gather_fusion.7 = bf16[256,128,128]{1,2,0:T(8,128)(2,1)} fusion(bf16[256,128,128]{1,2,0:T(8,128)(2,1)} %bitcast.113, s32[1024]{0:T(1024)S(1)} %get-tuple-element.24), kind=kCustom, calls=%fused_computation.7 | custom fusion | bytes 16778240 | tf_op jit(solution)/shard_map/gather | solution.py:99
  178.1 12.0 %copy.82 = bf16[4,2,32,128,128]{4,3,2,0,1:T(8,128)(2,1)} copy(bf16[4,2,32,128,128]{3,4,2,1,0:T(8,128)(2,1)} %bitcast.111) | data formatting | bytes 16777216 | tf_op jit(solution)/shard_map/convert_element_type | solution.py:113
  190.2 4.6 all-gather.6.cloned.1.call-done
  194.8 12.7 %gather_fusion.1 = bf16[256,128,128]{2,1,0:T(8,128)(2,1)} fusion(bf16[256,128,128]{2,1,0:T(8,128)(2,1)} %all-gather.6.cloned.1.call-done, s32[1024]{0:T(1024)S(1)} %pad_clamp_fusion.5), kind=kCustom, calls=%fused_computation.1 | custom fusion | bytes 16778240 | tf_op jit(solution)/shard_map/gather | solution.py:46
  207.4 10.7 %fusion.10 = bf16[128,32,128,1]{0,2,3,1:T(8,128)(2,1)S(1)} fusion(f32[32,128,128,1]{2,1,3,0:T(8,128)S(1)} %fusion.15, bf16[32,8,128,128]{3,2,1,0:T(8,128)(2,1)} %bitcast.108, bf16[128,32,8,128]{3,0,2,1:T(8,128)(2,1)} %bitcast.107), kind=kOutput, calls=%fused_computation.25 | convolution fusion | flops 1078984704 | bytes 19922944 | tf_op jit(solution)/shard_map/thkc,hkbc->thb/dot_general | solution.py:79
  218.2 9.1 %convolution_convert_fusion.1 = bf16[32,8,128,128]{3,2,1,0:T(8,128)(2,1)} fusion(bf16[128,32,8,128]{3,0,2,1:T(8,128)(2,1)} %bitcast.100, bf16[128,32,128,1]{0,2,3,1:T(8,128)(2,1)S(1)} %fusion.10), kind=kOutput, calls=%fused_computation.11 | convolution fusion | flops 1077936128 | bytes 17825792 | tf_op jit(solution)/shard_map/thkb,thc->hkbc/dot_general | solution.py:90
  227.2 12.3 %gather_fusion.6 = bf16[256,128,128]{2,1,0:T(8,128)(2,1)} fusion(bf16[256,128,128]{2,1,0:T(8,128)(2,1)} %bitcast.110, s32[1024]{0:T(1024)S(1)} %get-tuple-element.25), kind=kCustom, calls=%fused_computation.6 | custom fusion | bytes 16778240 | tf_op jit(solution)/shard_map/gather | solution.py:98
  239.5 10.4 %copy.79 = bf16[4,2,32,128,128]{4,3,2,0,1:T(8,128)(2,1)} copy(bf16[4,2,32,128,128]{4,3,2,1,0:T(8,128)(2,1)} %bitcast.112) | data formatting | bytes 16777216 | tf_op jit(solution)/shard_map/convert_element_type | solution.py:110
  250.2 11.6 %fusion.13 = f32[32,8,128,128]{3,2,1,0:T(8,128)} fusion(bf16[32,8,128,128]{3,2,1,0:T(8,128)(2,1)} %bitcast.109, f32[32,128,128,1]{2,1,3,0:T(8,128)S(1)} %fusion.15), kind=kOutput, calls=%fused_computation.48 | convolution fusion | flops 1076363264 | bytes 27262976 | tf_op jit(solution)/shard_map/thb,hkbc->thkc/dot_general | solution.py:70
  261.8 17.5 %copy.68 = f32[128,256,128]{2,0,1:T(8,128)} copy(f32[128,256,128]{0,2,1:T(8,128)} %bitcast.103) | data formatting | bytes 33554432 | tf_op jit(solution)/shard_map/reshape | solution.py:37
  282.2 52.5 %scatter_fusion = f32[128,64,128]{2,0,1:T(8,128)} fusion(f32[128,64,128]{2,0,1:T(8,128)} %broadcast.43.clone, s32[256]{0:T(256)S(1)} %bitcast.121, f32[256,128,128]{2,1,0:T(8,128)} %bitcast.102), kind=kCustom, calls=%fused_computation.8 | custom fusion | flops 4194304 | bytes 50332672 | tf_op jit(solution)/shard_map/scatter-add | solution.py:39
  340.3 11.5 %fusion.16 = f32[32,8,128,128]{3,2,1,0:T(8,128)} fusion(bf16[32,8,128,128]{3,2,1,0:T(8,128)(2,1)} %bitcast.98, bf16[128,32,128,1]{0,2,3,1:T(8,128)(2,1)S(1)} %fusion.10), kind=kOutput, calls=%fused_computation.50 | convolution fusion | flops 1073741824 | bytes 26214400 | tf_op jit(solution)/shard_map/thc,hkbc->thkb/dot_general | solution.py:83
  351.8 17.6 %copy.75 = f32[128,256,128]{2,0,1:T(8,128)} copy(f32[128,256,128]{0,2,1:T(8,128)} %bitcast.96) | data formatting | bytes 33554432 | tf_op jit(solution)/shard_map/reshape | solution.py:37
  371.9 51.3 %scatter_fusion.1 = f32[128,64,128]{2,0,1:T(8,128)} fusion(f32[128,64,128]{2,0,1:T(8,128)} %broadcast.43.clone.1, s32[256]{0:T(256)S(1)} %bitcast.119, f32[256,128,128]{2,1,0:T(8,128)} %bitcast.101), kind=kCustom, calls=%fused_computation.9 | custom fusion | flops 4194304 | bytes 50332672 | tf_op jit(solution)/shard_map/scatter-add | solution.py:39
  432.2 40.6 %reduce-scatter.7.cloned.1.call-done = bf16[128,2048]{0,1:T(8,128)(2,1)} async-done(((bf16[128,8192]{0,1:T(8,128)(2,1)}), bf16[128,2048]{0,1:T(8,128)(2,1)}) %reduce-scatter.7.cloned.1.call-update) | async-done | bytes 524304 | tf_op jit(solution)/shard_map/reduce_scatter | solution.py:87
  474.9 31.9 %all-gather.14.cloned.1.call-done = bf16[64,128,128]{2,1,0:T(8,128)(2,1)} async-done(((bf16[32,128,128]{2,1,0:T(8,128)(2,1)}), bf16[64,128,128]{2,1,0:T(8,128)(2,1)}) %all-gather.14.cloned.1.call-update) | async-done | bytes 2097168 | tf_op jit(solution)/shard_map/all_gather | solution.py:120
  506.7 4.1 convert_element_type.79
  510.9 30.5 %all-gather.12.cloned.1.call-done = bf16[64,128,128]{2,1,0:T(8,128)(2,1)} async-done(((bf16[32,128,128]{2,1,0:T(8,128)(2,1)}), bf16[64,128,128]{2,1,0:T(8,128)(2,1)}) %all-gather.12.cloned.1.call-update) | async-done | bytes 2097168 | tf_op jit(solution)/shard_map/all_gather | solution.py:117
  541.4 4.1 convert_element_type.73
  (75 shorter events, 45.6 us)
Async XLA Ops:
  7.2 19.9 %copy-start = (s32[256,1]{0,1:T(1,128)S(1)}, s32[256,1]{0,1:T(1,128)}, u32[]{:S(2)}) copy-start(s32[256,1]{0,1:T(1,128)} %param.15) | copy-start | bytes 3076
  7.2 3.7 copy-start.3
  7.2 7.1 %copy-start.4 = (s32[256,1]{0,1:T(1,128)S(1)}, s32[256,1]{0,1:T(1,128)}, u32[]{:S(2)}) copy-start(s32[256,1]{0,1:T(1,128)} %param.14) | copy-start | bytes 3076
  7.2 13.5 %copy-start.5 = (s32[256,1]{0,1:T(1,128)S(1)}, s32[256,1]{0,1:T(1,128)}, u32[]{:S(2)}) copy-start(s32[256,1]{0,1:T(1,128)} %param.13) | copy-start | bytes 3076
  7.2 28.2 %copy-start.2 = (s32[256,1]{0,1:T(1,128)S(1)}, s32[256,1]{0,1:T(1,128)}, u32[]{:S(2)}) copy-start(s32[256,1]{0,1:T(1,128)} %param.12) | copy-start | bytes 3076
  7.2 91.5 %all-gather.10.cloned.1.call-start = ((), (), s32[]{:S(2)}) async-start(), calls=%async_computation.6 | async-start | bytes 2621440 | tf_op jit(solution)/shard_map/all_gather | solution.py:59
  9.4 125.5 %all-gather.8.cloned.1.call-start = ((), (), s32[]{:S(2)}) async-start(), calls=%async_computation.5 | async-start | bytes 10485760 | tf_op jit(solution)/shard_map/all_gather | solution.py:61
  10.1 184.6 %all-gather.6.cloned.1.call-start = ((), (), s32[]{:S(2)}) async-start(), calls=%async_computation.4 | async-start | bytes 10485760 | tf_op jit(solution)/shard_map/all_gather | solution.py:68
  10.9 417.9 %reduce-scatter.11.cloned.1.call-start = ((), (), s32[]{:S(2)}) async-start(), calls=%async_computation.11 | async-start | bytes 9437184 | tf_op jit(solution)/shard_map/reduce_scatter | solution.py:112
  11.2 18.5 %collective-permute-start = (bf16[128,2048]{0,1:T(8,128)(2,1)S(1)}, bf16[128,2048]{0,1:T(8,128)(2,1)S(1)}, u32[]{:S(2)}, u32[]{:S(2)}) collective-permute-start(bf16[128,2048]{0,1:T(8,128)(2,1)S(1)} %copy.70), channel_id=1, source_target_pairs={{0,1},{1,2},{2,3},{3,0},{4,5},{5,6},{6,7},{7,4},{8,9},{9,10},{10,1... | collective-permute-start | bytes 1572872 | tf_op jit(solution)/shard_map/ppermute | solution.py:16
  29.7 30.5 %collective-permute-start.1 = (bf16[128,2048]{0,1:T(8,128)(2,1)S(1)}, bf16[128,2048]{0,1:T(8,128)(2,1)S(1)}, u32[]{:S(2)}, u32[]{:S(2)}) collective-permute-start(bf16[128,2048]{0,1:T(8,128)(2,1)S(1)} %collective-permute-done), channel_id=1, source_target_pairs={{0,1},{1,2},{2,3},{3,0},{4,5},{5,6},{6,7},{7,4},{8,9},{9,10},{10,1... | collective-permute-start | bytes 1572872 | tf_op jit(solution)/shard_map/ppermute | solution.py:16
  60.2 24.3 %collective-permute-start.2 = (bf16[128,2048]{0,1:T(8,128)(2,1)S(1)}, bf16[128,2048]{0,1:T(8,128)(2,1)S(1)}, u32[]{:S(2)}, u32[]{:S(2)}) collective-permute-start(bf16[128,2048]{0,1:T(8,128)(2,1)S(1)} %collective-permute-done.1), channel_id=1, source_target_pairs={{0,1},{1,2},{2,3},{3,0},{4,5},{5,6},{6,7},{7,4},{8,9},{9,10},{10,1... | collective-permute-start | bytes 1572872 | tf_op jit(solution)/shard_map/ppermute | solution.py:16
  190.1 239.4 %reduce-scatter.9.cloned.1.call-start = ((), (), s32[]{:S(2)}) async-start(), calls=%async_computation.9 | async-start | bytes 9437184 | tf_op jit(solution)/shard_map/reduce_scatter | solution.py:109
  249.9 180.3 %reduce-scatter.5.cloned.1.call-start = ((), (), s32[]{:S(2)}) async-start(), calls=%async_computation.7 | async-start | bytes 2621440 | tf_op jit(solution)/shard_map/reduce_scatter | solution.py:74
  340.2 132.6 %reduce-scatter.7.cloned.1.call-start = ((), (), s32[]{:S(2)}) async-start(), calls=%async_computation.8 | async-start | bytes 2621440 | tf_op jit(solution)/shard_map/reduce_scatter | solution.py:87
  428.7 78.0 %all-gather.14.cloned.1.call-start = ((), (), s32[]{:S(2)}) async-start(), calls=%async_computation.12 | async-start | bytes 3145728 | tf_op jit(solution)/shard_map/all_gather | solution.py:120
  429.4 112.0 %all-gather.12.cloned.1.call-start = ((), (), s32[]{:S(2)}) async-start(), calls=%async_computation.10 | async-start | bytes 3145728 | tf_op jit(solution)/shard_map/all_gather | solution.py:117
  506.7 38.8 %copy-start.1 = (s32[256,1]{0,1:T(1,128)S(1)}, s32[256,1]{0,1:T(1,128)}, u32[]{:S(2)}) copy-start(s32[256,1]{0,1:T(1,128)} %param.15) | copy-start | bytes 3076
Sparse Core Ops, SparseCore 0:
  10.2 65.2 all-gather.9
  77.1 57.7 all-gather.7
  136.5 58.2 all-gather.5
  198.1 71.4 reduce-scatter.10
  272.9 71.4 reduce-scatter.8
  347.2 43.6 reduce-scatter.4
  428.8 43.9 reduce-scatter.6
  474.4 32.3 all-gather.13
  508.3 33.0 all-gather.11
